TPU v7x, 256 devices: a whole 4x4x8 slice. The times are simulated.
256 devices in a mesh: seq: 32 (over x, z), ch: 8 (over y, core).
Axes of the slice: x: 4, y: 4, z: 8, core: 2. Of those that a mesh axis runs over, the one named last changes fastest.
Arguments:
- out_gate: bfloat16 [12288, 4096], P('seq', 'ch'), may hold values from -6 to 6
- in_gate: bfloat16 [12288, 4096], P('seq', 'ch'), may hold values from -6 to 6
- values: bfloat16 [12288, 4096], P('seq', 'ch'), may hold values from -6 to 6
- short_filter: float32 [3, 3, 4096], P(None, None, 'ch'), may hold values from -3 to 3
- long_filter: float32 [12288, 4096], P('seq', 'ch'), may hold values from -1.5 to 1.5
- skip_gain: float32 [4096], P('ch'), may hold values from -4 to 4
- out_weight: bfloat16 [4096, 4096], P(None, 'ch'), may hold values from -0.09375 to 0.09375
Outputs:
- projected: bfloat16 [12288, 4096], P('seq', 'ch')
All inputs are finite; a program needn't handle non-finite values.
Results may differ from a plain program's by a relative error of at most 0.0049.
Values may be sent and summed in bfloat16 or wider, within the bound.
A program may use at most 128 MiB of HBM per device.

v0:
```python
import math
import jax
import jax.numpy as jnp
from jax import lax
from jax.sharding import PartitionSpec as P

highest = lax.Precision.HIGHEST


def shifted(block, axis, distance):
    devices = range(lax.axis_size(axis))
    route = [(i - distance, i) for i in devices if i - distance in devices]
    return lax.ppermute(block, axis, route)


def phase_table(row_ids, col_ids, modulus, direction):
    product = row_ids[:, None] * col_ids[None, :] % modulus
    angles = product.astype(jnp.float32) * (direction * 2.0 * math.pi / modulus)
    return (jnp.cos(angles), jnp.sin(angles))


def contract(pattern, first_op, second_op):
    return jnp.einsum(pattern, first_op, second_op, precision=highest)


def complex_apply(pattern, phases, operand):
    cosine, sine_part = phases
    real_part, imaginary = operand
    return (
        contract(pattern, cosine, real_part) - contract(pattern, sine_part, imaginary),
        contract(pattern, cosine, imaginary) + contract(pattern, sine_part, real_part),
    )


def complex_times(first_op, second_op):
    return (
        first_op[0] * second_op[0] - first_op[1] * second_op[1],
        first_op[0] * second_op[1] + first_op[1] * second_op[0],
    )


def sequence_conv(mixed_in, long_filter):
    seq_count = lax.axis_size("seq")
    seq_index = lax.axis_index("seq")
    row_count = mixed_in.shape[0]
    total_len = row_count * seq_count
    piece_rows = row_count // seq_count
    rows_b = jnp.arange(row_count, dtype=jnp.int32)
    device_ids = jnp.arange(seq_count, dtype=jnp.int32)
    positions = seq_index * row_count + rows_b
    angles = positions.astype(jnp.float32) * (math.pi / total_len)
    cosines = jnp.cos(angles)[:, None]
    sines = jnp.sin(angles)[:, None]
    planes = jnp.stack([mixed_in, long_filter])[:, None]
    spread = lax.all_to_all(planes, "seq", split_axis=2, concat_axis=1, tiled=True)
    local_b = seq_index * piece_rows + jnp.arange(piece_rows, dtype=jnp.int32)
    arrived_pos = device_ids[:, None] * row_count + local_b[None, :]
    arrived_angles = arrived_pos.astype(jnp.float32) * (math.pi / total_len)
    arrived_cos = jnp.cos(arrived_angles)[:, :, None]
    arrived_sin = jnp.sin(arrived_angles)[:, :, None]
    zeros_plane = jnp.zeros_like(spread[0])
    real_part = jnp.stack([spread[0], spread[0] * arrived_cos, spread[1], spread[1] * arrived_cos])
    imaginary = jnp.stack(
        [zeros_plane, -spread[0] * arrived_sin, zeros_plane, -spread[1] * arrived_sin]
    )
    sectioned = complex_apply(
        "kp,xpbc->xkbc",
        phase_table(device_ids, device_ids, seq_count, -1.0),
        (real_part, imaginary),
    )
    twist_table = phase_table(device_ids, local_b, total_len, -1.0)
    sectioned = complex_times(sectioned, (twist_table[0][:, :, None], twist_table[1][:, :, None]))
    arrived = (
        lax.all_to_all(sectioned[0], "seq", split_axis=1, concat_axis=2, tiled=True),
        lax.all_to_all(sectioned[1], "seq", split_axis=1, concat_axis=2, tiled=True),
    )
    spectra = complex_apply("mb,xkbc->xkmc", phase_table(rows_b, rows_b, row_count, -1.0), arrived)
    product = complex_times((spectra[0][:2], spectra[1][:2]), (spectra[0][2:], spectra[1][2:]))
    sectioned = complex_apply("mb,xkmc->xkbc", phase_table(rows_b, rows_b, row_count, 1.0), product)
    twist_table = phase_table(seq_index.reshape(1), rows_b, total_len, 1.0)
    sectioned = complex_times(sectioned, (twist_table[0][:, :, None], twist_table[1][:, :, None]))
    returned = (
        lax.all_to_all(sectioned[0], "seq", split_axis=2, concat_axis=1, tiled=True),
        lax.all_to_all(sectioned[1], "seq", split_axis=2, concat_axis=1, tiled=True),
    )
    sectioned = complex_apply(
        "kp,xkbc->xpbc", phase_table(device_ids, device_ids, seq_count, 1.0), returned
    )
    restored = (
        lax.all_to_all(sectioned[0], "seq", split_axis=1, concat_axis=2, tiled=True),
        lax.all_to_all(sectioned[1], "seq", split_axis=1, concat_axis=2, tiled=True),
    )
    real_out = restored[0][:, 0] / total_len
    imag_out = restored[1][:, 0] / total_len
    return 0.5 * (real_out[0] + cosines * real_out[1] - sines * imag_out[1])


def on_device(out_gate, in_gate, values, short_filter, long_filter, skip_gain, out_weight):
    tap_count = short_filter.shape[1]
    row_count = out_gate.shape[0]
    stacked = jnp.stack([out_gate, in_gate, values])
    rim_rows = shifted(stacked[:, row_count - (tap_count - 1) :], "seq", 1)
    widened = jnp.concatenate([rim_rows, stacked], axis=1).astype(jnp.float32)
    shorted = short_filter[:, 0, None, :] * widened[:, tap_count - 1 :]
    for offset in range(1, tap_count):
        start_row = tap_count - 1 - offset
        shorted = (
            shorted
            + short_filter[:, offset, None, :] * widened[:, start_row : start_row + row_count]
        )
    gate_late = shorted[0]
    mixed_in = shorted[1] * shorted[2]
    long_out = sequence_conv(mixed_in, long_filter)
    filtered = long_out + skip_gain * mixed_in
    mixed = (gate_late * filtered).astype(jnp.bfloat16)
    summed = jnp.dot(
        lax.all_gather(mixed, "ch", axis=1, tiled=True),
        out_weight,
        preferred_element_type=jnp.float32,
    )
    return summed.astype(jnp.bfloat16)


def solution(mesh):
    return jax.shard_map(
        on_device,
        mesh=mesh,
        in_specs=(
            P("seq", "ch"),
            P("seq", "ch"),
            P("seq", "ch"),
            P(None, None, "ch"),
            P("seq", "ch"),
            P("ch"),
            P(None, "ch"),
        ),
        out_specs=P("seq", "ch"),
        check_vma=False,
    )
```

profile of v0, /device:TPU:1, one launch (start us, length us, event | category | flops | bytes accessed | tf_op | source)
XLA Modules:
  0.0 544.4 jit_solution(16303291833496536461)
XLA Ops:
  6.5 0.7 pad_maximum_fusion.6
  7.3 4.4 collective-permute-start
  11.7 0.9 fusion.196
  12.6 1.6 maximum_convert_fusion
  14.2 0.7 fusion.4
  14.9 0.1 slice_multiply_fusion.4
  15.0 1.5 copy-done.5
  16.6 0.1 maximum_bitcast_fusion
  16.7 2.4 copy.68
  19.1 12.4 %all-to-all-start = ((f32[2,1,384,512]{3,0,1,2:T(2,128)}), f32[2,1,384,512]{3,0,1,2:T(2,128)S(1)}, u32[]{:S(2)}, u32[]{:S(2)}) async-start(f32[2,1,384,512]{3,0,1,2:T(2,128)} %copy.68), calls=%async_computation | async-start | bytes 3145728 | tf_op jit(solution)/shard_map/all_to_all | solution.py:55
  31.6 0.1 fusion.108
  31.7 36.7 %all-to-all-done = f32[2,1,384,512]{3,0,1,2:T(2,128)S(1)} async-done(((f32[2,1,384,512]{3,0,1,2:T(2,128)}), f32[2,1,384,512]{3,0,1,2:T(2,128)S(1)}, u32[]{:S(2)}, u32[]{:S(2)}) %all-to-all-start) | async-done | bytes 1572896 | tf_op jit(solution)/shard_map/all_to_all | solution.py:55
  68.4 1.2 fusion.193
  69.6 0.3 fusion.194
  69.9 0.3 fusion.195
  70.3 0.1 broadcast.249
  70.4 3.3 fusion.3
  73.7 3.3 fusion.2
  76.9 3.6 convolution_subtract_fusion
  80.6 6.0 %fusion = (f32[4,32,12,512]{3,1,2,0:T(8,128)S(1)}, f32[4,32,12,512]{3,1,2,0:T(8,128)}) fusion(f32[4,12,512,32]{2,3,1,0:T(8,128)S(1)} %convolution_subtract_fusion, f32[32,12]{0,1:T(8,128)S(1)} %get-tuple-element.27, f32[32,12]{0,1:T(8,128)S(1)} %get-tuple-element.26, f32[4,12,512,32]{2,3,1,0:T(8,128)S(1)} %fusion.2, ...), kind=kOutput, calls=%fused_computation.4 | convolution fusion | flops 309868544 | bytes 15731712 | tf_op jit(solution)/shard_map/kp,xpbc->xkbc/dot_general | solution.py:23
  86.5 3.7 copy.79
  90.3 7.3 %all-to-all-start.1 = ((f32[4,32,12,512]{3,0,2,1:T(4,128)}), f32[4,32,12,512]{3,0,2,1:T(4,128)S(1)}, u32[]{:S(2)}, u32[]{:S(2)}) async-start(f32[4,32,12,512]{3,0,2,1:T(4,128)} %copy.79), calls=%async_computation.1 | async-start | bytes 6291456 | tf_op jit(solution)/shard_map/all_to_all | solution.py:74
  97.6 5.5 %copy.81 = f32[4,32,12,512]{3,0,2,1:T(4,128)} copy(f32[4,32,12,512]{3,1,2,0:T(8,128)} %get-tuple-element.8) | data formatting | bytes 6291456 | tf_op jit(solution)/shard_map/add | solution.py:38
  103.1 65.8 %all-to-all-done.1 = f32[4,32,12,512]{3,0,2,1:T(4,128)S(1)} async-done(((f32[4,32,12,512]{3,0,2,1:T(4,128)}), f32[4,32,12,512]{3,0,2,1:T(4,128)S(1)}, u32[]{:S(2)}, u32[]{:S(2)}) %all-to-all-start.1) | async-done | bytes 3145760 | tf_op jit(solution)/shard_map/all_to_all | solution.py:74
  168.9 1.7 copy-done.3
  170.6 7.8 %all-to-all-start.2 = ((f32[4,32,12,512]{3,0,2,1:T(4,128)}), f32[4,32,12,512]{3,0,2,1:T(4,128)}, u32[]{:S(2)}, u32[]{:S(2)}) async-start(f32[4,32,12,512]{3,0,2,1:T(4,128)} %copy.81), calls=%async_computation.2 | async-start | bytes 6291456 | tf_op jit(solution)/shard_map/all_to_all | solution.py:75
  178.5 3.2 copy.80
  181.7 9.8 %fusion.43 = f32[4,512,384]{2,1,0:T(8,128)} fusion(f32[4,384,512]{1,2,0:T(8,128)S(1)} %copy.80), kind=kOutput, calls=%fused_computation.73 | convolution fusion | flops 3625205760 | bytes 6291456 | tf_op jit(solution)/shard_map/mb,xkbc->xkmc/dot_general | solution.py:23
  191.5 60.2 %all-to-all-done.2 = f32[4,32,12,512]{3,0,2,1:T(4,128)} async-done(((f32[4,32,12,512]{3,0,2,1:T(4,128)}), f32[4,32,12,512]{3,0,2,1:T(4,128)}, u32[]{:S(2)}, u32[]{:S(2)}) %all-to-all-start.2) | async-done | bytes 3145760 | tf_op jit(solution)/shard_map/all_to_all | solution.py:75
  251.7 5.2 copy.82
  256.8 10.7 %fusion.41 = f32[4,512,384]{2,1,0:T(8,128)S(1)} fusion(f32[4,384,512]{1,2,0:T(8,128)} %copy.82), kind=kOutput, calls=%fused_computation.71 | convolution fusion | flops 3625205760 | bytes 6291456 | tf_op jit(solution)/shard_map/mb,xkbc->xkmc/dot_general | solution.py:23
  267.6 9.2 %subtract_bitcast_fusion = f32[4,1,384,512]{2,3,0,1:T(8,128)S(1)} fusion(f32[4,512,384]{2,1,0:T(8,128)S(1)} %copy-done.4, f32[4,384,512]{1,2,0:T(8,128)S(1)} %copy-done), kind=kOutput, calls=%fused_computation.9 | convolution fusion | flops 3625992192 | bytes 9437184 | tf_op jit(solution)/shard_map/mb,xkbc->xkmc/dot_general | solution.py:23
  276.8 9.0 %add_bitcast_fusion = f32[4,1,384,512]{2,3,0,1:T(8,128)S(1)} fusion(f32[4,512,384]{2,1,0:T(8,128)S(1)} %fusion.41, f32[4,384,512]{1,2,0:T(8,128)S(1)} %copy.80), kind=kOutput, calls=%fused_computation.8 | convolution fusion | flops 3625992192 | bytes 9437184 | tf_op jit(solution)/shard_map/mb,xkbc->xkmc/dot_general | solution.py:23
  285.8 0.3 multiply_subtract_fusion
  286.1 5.4 fusion.12
  291.5 5.8 %fusion.10 = f32[2,512,384]{2,1,0:T(8,128)S(1)} fusion(f32[2,1,384,512]{2,3,0,1:T(8,128)S(1)} %get-tuple-element.10), kind=kOutput, calls=%fused_computation.28 | convolution fusion | flops 1813266432 | bytes 3145728 | tf_op jit(solution)/shard_map/mb,xkmc->xkbc/dot_general | solution.py:23
  297.3 5.4 fusion.18
  302.8 5.5 %fusion.7 = (f32[2,1,384,512]{2,3,0,1:T(8,128)S(1)}, f32[2,1,384,512]{2,3,0,1:T(8,128)S(1)}) fusion(f32[2,512,384]{2,1,0:T(8,128)S(1)} %fusion.18, f32[384]{0:T(512)S(1)} %get-tuple-element.32, f32[384]{0:T(512)S(1)} %get-tuple-element.33, f32[2,512,384]{2,1,0:T(8,128)S(1)} %fusion.10, f32[2,1,384,512]{2,3,0,1:T(8,128)S(1)} %get-tuple-element.9), kind=kOutput, calls=%fused_computation.23 | convolution fusion | flops 1816018944 | bytes 7867392 | tf_op jit(solution)/shard_map/mb,xkmc->xkbc/dot_general | solution.py:23
  308.3 2.1 copy.85
  310.4 5.9 %all-to-all-start.3 = ((f32[2,1,384,512]{3,0,1,2:T(2,128)}), f32[2,1,384,512]{3,0,1,2:T(2,128)S(1)}, u32[]{:S(2)}, u32[]{:S(2)}) async-start(f32[2,1,384,512]{3,0,1,2:T(2,128)} %copy.85), calls=%async_computation.3 | async-start | bytes 3145728 | tf_op jit(solution)/shard_map/all_to_all | solution.py:83
  316.2 2.1 copy.87
  318.3 34.6 %all-to-all-done.3 = f32[2,1,384,512]{3,0,1,2:T(2,128)S(1)} async-done(((f32[2,1,384,512]{3,0,1,2:T(2,128)}), f32[2,1,384,512]{3,0,1,2:T(2,128)S(1)}, u32[]{:S(2)}, u32[]{:S(2)}) %all-to-all-start.3) | async-done | bytes 1572896 | tf_op jit(solution)/shard_map/all_to_all | solution.py:83
  352.9 7.7 %all-to-all-start.4 = ((f32[2,1,384,512]{3,0,1,2:T(2,128)}), f32[2,1,384,512]{3,0,1,2:T(2,128)S(1)}, u32[]{:S(2)}, u32[]{:S(2)}) async-start(f32[2,1,384,512]{3,0,1,2:T(2,128)} %copy.87), calls=%async_computation.4 | async-start | bytes 3145728 | tf_op jit(solution)/shard_map/all_to_all | solution.py:84
  360.7 3.7 fusion.28
  364.3 33.1 %all-to-all-done.4 = f32[2,1,384,512]{3,0,1,2:T(2,128)S(1)} async-done(((f32[2,1,384,512]{3,0,1,2:T(2,128)}), f32[2,1,384,512]{3,0,1,2:T(2,128)S(1)}, u32[]{:S(2)}, u32[]{:S(2)}) %all-to-all-start.4) | async-done | bytes 1572896 | tf_op jit(solution)/shard_map/all_to_all | solution.py:84
  397.5 4.0 subtract_bitcast_fusion.1
  401.5 2.4 copy.89
  403.9 7.8 %all-to-all-start.5 = ((f32[2,32,12,512]{3,0,2,1:T(2,128)}), f32[2,32,12,512]{3,0,2,1:T(2,128)}, u32[]{:S(2)}, u32[]{:S(2)}) async-start(f32[2,32,12,512]{3,0,2,1:T(2,128)} %copy.89), calls=%async_computation.5 | async-start | bytes 3145728 | tf_op jit(solution)/shard_map/all_to_all | solution.py:90
  411.6 2.5 fusion.24
  414.2 2.6 add_bitcast_fusion.1
  416.8 2.4 copy.92
  419.2 29.2 %all-to-all-done.5 = f32[2,32,12,512]{3,0,2,1:T(2,128)} async-done(((f32[2,32,12,512]{3,0,2,1:T(2,128)}), f32[2,32,12,512]{3,0,2,1:T(2,128)}, u32[]{:S(2)}, u32[]{:S(2)}) %all-to-all-start.5) | async-done | bytes 1572896 | tf_op jit(solution)/shard_map/all_to_all | solution.py:90
  448.4 7.8 %all-to-all-start.6 = ((f32[2,32,12,512]{3,0,2,1:T(2,128)}), f32[2,32,12,512]{3,0,2,1:T(2,128)}, u32[]{:S(2)}, u32[]{:S(2)}) async-start(f32[2,32,12,512]{3,0,2,1:T(2,128)} %copy.92), calls=%async_computation.6 | async-start | bytes 3145728 | tf_op jit(solution)/shard_map/all_to_all | solution.py:91
  456.2 0.3 all-gather.2.cloned.1.call-start
  456.5 2.3 broadcast_multiply_fusion
  458.8 4.1 slice_reduce_fusion
  463.0 1.0 squeeze.10
  464.0 1.0 squeeze.9
  464.9 28.1 %all-to-all-done.6 = f32[2,32,12,512]{3,0,2,1:T(2,128)} async-done(((f32[2,32,12,512]{3,0,2,1:T(2,128)}), f32[2,32,12,512]{3,0,2,1:T(2,128)}, u32[]{:S(2)}, u32[]{:S(2)}) %all-to-all-start.6) | async-done | bytes 1572896 | tf_op jit(solution)/shard_map/all_to_all | solution.py:91
  493.0 4.0 fusion.30
  497.0 1.0 squeeze.11
  498.0 2.7 fusion.32
  500.7 31.0 %all-gather.2.cloned.1.call-done = bf16[384,4096]{1,0:T(8,128)(2,1)} async-done(((bf16[384,512]{1,0:T(8,128)(2,1)}), bf16[384,4096]{1,0:T(8,128)(2,1)}) %all-gather.2.cloned.1.call-update) | async-done | bytes 3145744 | tf_op jit(solution)/shard_map/all_gather | solution.py:117
  531.6 5.7 %convolution_convert_fusion = bf16[384,512]{1,0:T(8,128)(2,1)} fusion(bf16[384,4096]{1,0:T(8,128)(2,1)} %all-gather.2.cloned.1.call-done, bf16[4096,512]{1,0:T(8,128)(2,1)} %param.13), kind=kOutput, calls=%fused_computation.48 | convolution fusion | flops 1610809344 | bytes 7733248 | tf_op jit(solution)/shard_map/dot_general | solution.py:116
  (20 shorter events, 0.2 us)
Async XLA Ops:
  7.3 5.3 collective-permute-start
  14.9 1.8 copy-start.1
  14.9 1.7 copy-start.5
  19.1 49.3 %all-to-all-start = ((f32[2,1,384,512]{3,0,1,2:T(2,128)}), f32[2,1,384,512]{3,0,1,2:T(2,128)S(1)}, u32[]{:S(2)}, u32[]{:S(2)}) async-start(f32[2,1,384,512]{3,0,1,2:T(2,128)} %copy.68), calls=%async_computation | async-start | bytes 3145728 | tf_op jit(solution)/shard_map/all_to_all | solution.py:55
  90.3 78.6 %all-to-all-start.1 = ((f32[4,32,12,512]{3,0,2,1:T(4,128)}), f32[4,32,12,512]{3,0,2,1:T(4,128)S(1)}, u32[]{:S(2)}, u32[]{:S(2)}) async-start(f32[4,32,12,512]{3,0,2,1:T(4,128)} %copy.79), calls=%async_computation.1 | async-start | bytes 6291456 | tf_op jit(solution)/shard_map/all_to_all | solution.py:74
  168.9 1.7 copy-start.3
  170.6 81.0 %all-to-all-start.2 = ((f32[4,32,12,512]{3,0,2,1:T(4,128)}), f32[4,32,12,512]{3,0,2,1:T(4,128)}, u32[]{:S(2)}, u32[]{:S(2)}) async-start(f32[4,32,12,512]{3,0,2,1:T(4,128)} %copy.81), calls=%async_computation.2 | async-start | bytes 6291456 | tf_op jit(solution)/shard_map/all_to_all | solution.py:75
  256.8 10.7 %copy-start = (f32[4,384,512]{1,2,0:T(8,128)S(1)}, f32[4,384,512]{1,2,0:T(8,128)}, u32[]{:S(2)}) copy-start(f32[4,384,512]{1,2,0:T(8,128)} %copy.82) | copy-start | bytes 9437188
  256.8 10.7 %copy-start.4 = (f32[4,512,384]{2,1,0:T(8,128)S(1)}, f32[4,512,384]{2,1,0:T(8,128)}, u32[]{:S(2)}) copy-start(f32[4,512,384]{2,1,0:T(8,128)} %fusion.43) | copy-start | bytes 9437188
  310.4 42.6 %all-to-all-start.3 = ((f32[2,1,384,512]{3,0,1,2:T(2,128)}), f32[2,1,384,512]{3,0,1,2:T(2,128)S(1)}, u32[]{:S(2)}, u32[]{:S(2)}) async-start(f32[2,1,384,512]{3,0,1,2:T(2,128)} %copy.85), calls=%async_computation.3 | async-start | bytes 3145728 | tf_op jit(solution)/shard_map/all_to_all | solution.py:83
  352.9 44.5 %all-to-all-start.4 = ((f32[2,1,384,512]{3,0,1,2:T(2,128)}), f32[2,1,384,512]{3,0,1,2:T(2,128)S(1)}, u32[]{:S(2)}, u32[]{:S(2)}) async-start(f32[2,1,384,512]{3,0,1,2:T(2,128)} %copy.87), calls=%async_computation.4 | async-start | bytes 3145728 | tf_op jit(solution)/shard_map/all_to_all | solution.py:84
  403.9 44.6 %all-to-all-start.5 = ((f32[2,32,12,512]{3,0,2,1:T(2,128)}), f32[2,32,12,512]{3,0,2,1:T(2,128)}, u32[]{:S(2)}, u32[]{:S(2)}) async-start(f32[2,32,12,512]{3,0,2,1:T(2,128)} %copy.89), calls=%async_computation.5 | async-start | bytes 3145728 | tf_op jit(solution)/shard_map/all_to_all | solution.py:90
  448.4 44.6 %all-to-all-start.6 = ((f32[2,32,12,512]{3,0,2,1:T(2,128)}), f32[2,32,12,512]{3,0,2,1:T(2,128)}, u32[]{:S(2)}, u32[]{:S(2)}) async-start(f32[2,32,12,512]{3,0,2,1:T(2,128)} %copy.92), calls=%async_computation.6 | async-start | bytes 3145728 | tf_op jit(solution)/shard_map/all_to_all | solution.py:91
  456.2 75.4 %all-gather.2.cloned.1.call-start = ((), (), s32[]{:S(2)}) async-start(), calls=%async_computation.7 | async-start | bytes 3538944 | tf_op jit(solution)/shard_map/all_gather | solution.py:117
  464.0 34.0 %copy-start.2 = (f32[3,384,512]{2,1,0:T(8,128)S(1)}, f32[3,384,512]{2,1,0:T(8,128)}, u32[]{:S(2)}) copy-start(f32[3,384,512]{2,1,0:T(8,128)} %copy-done.1) | copy-start | bytes 7077892
  464.0 34.0 %copy-start.6 = (f32[512]{0:T(512)S(1)}, f32[512]{0:T(512)}, u32[]{:S(2)}) copy-start(f32[512]{0:T(512)} %param.12) | copy-start | bytes 6148
Sparse Core Ops, SparseCore 0:
  500.8 30.8 all-gather.1
where the time goes:
time: 548 us; the launch traced here: 544 us
  waiting for transfers between devices  319 us (58%)
  matrix products  95.5 us (17%)
  starting transfers between devices  61.3 us (11%)
  local copies, waits for them, and re-layouts  41.5 us (8%)
  between operations  14 us (3%)
  other arithmetic  13.5 us (2%)
    all_to_all x2, waiting for transfers between devices, sequence_conv(): lax.all_to_all(sectioned[0], 'seq', split_axis=1, concat_axis=2, tiled=True)  95 us
    dot_general x16, matrix products, contract(): return jnp.einsum(pattern, first_op, second_op, precision=highest)  89.8 us
    all_to_all x2, waiting for transfers between devices, sequence_conv(): lax.all_to_all(sectioned[1], 'seq', split_axis=1, concat_axis=2, tiled=True)  88.2 us
    all_to_all x1, waiting for transfers between devices, sequence_conv(): lax.all_to_all(planes, 'seq', split_axis=2, concat_axis=1, tiled=True)  36.7 us
    all_to_all x1, waiting for transfers between devices, sequence_conv(): lax.all_to_all(sectioned[0], 'seq', split_axis=2, concat_axis=1, tiled=True)  34.6 us
    all_to_all x1, waiting for transfers between devices, sequence_conv(): lax.all_to_all(sectioned[1], 'seq', split_axis=2, concat_axis=1, tiled=True)  33.1 us
    all_gather x1, waiting for transfers between devices, on_device(): lax.all_gather(mixed, 'ch', axis=1, tiled=True)  31 us
    all_to_all x2, starting transfers between devices, sequence_conv(): lax.all_to_all(sectioned[1], 'seq', split_axis=1, concat_axis=2, tiled=True)  15.6 us
  transfers between devices with their start and end apart: 9, of which 8 were waited for; matrix products, arithmetic and copies ran while one was open for 8% of the time, Pallas kernels for 0%

commit v1 on v0

--- a/solution.py
+++ b/solution.py
@@ -96,6 +96,28 @@
 
 
 def on_device(out_gate, in_gate, values, short_filter, long_filter, skip_gain, out_weight):
+
+    def cards_connect(u_in, across):
+        part_now = lax.axis_size(across)
+        m_next, val, left_arr = (part_now, lax.axis_index(across), u_in.shape[1])
+        pool = tuple(((ix, (ix + 1) % m_next) for ix in range(m_next)))
+        ledger = tuple(((ix, (ix - 1) % m_next) for ix in range(m_next)))
+        block_next = jnp.zeros((*u_in.shape[:1], m_next * left_arr, *u_in.shape[2:]), u_in.dtype)
+        spare = oldest = u_in
+        item_now = m_next // 2
+        block_next = lax.dynamic_update_slice_in_dim(block_next, u_in, val * left_arr, axis=1)
+        for dd in range(1, item_now + 1):
+            spare = lax.ppermute(spare, axis_name=across, perm=pool)
+            block_next = lax.dynamic_update_slice_in_dim(
+                block_next, spare, (val - dd) % m_next * left_arr, axis=1
+            )
+            if dd < m_next - item_now:
+                oldest = lax.ppermute(oldest, axis_name=across, perm=ledger)
+                block_next = lax.dynamic_update_slice_in_dim(
+                    block_next, oldest, (val + dd) % m_next * left_arr, axis=1
+                )
+        return block_next
+
     tap_count = short_filter.shape[1]
     row_count = out_gate.shape[0]
     stacked = jnp.stack([out_gate, in_gate, values])
@@ -114,9 +136,7 @@
     filtered = long_out + skip_gain * mixed_in
     mixed = (gate_late * filtered).astype(jnp.bfloat16)
     summed = jnp.dot(
-        lax.all_gather(mixed, "ch", axis=1, tiled=True),
-        out_weight,
-        preferred_element_type=jnp.float32,
+        cards_connect(mixed, across="ch"), out_weight, preferred_element_type=jnp.float32
     )
     return summed.astype(jnp.bfloat16)
 

time: 548 us -> 541 us (0.987)
  waiting for transfers between devices: 319 us -> 301 us
  between operations: 14 us -> 0.67 us
  starting transfers between devices: 61.3 us -> 74.6 us
  local copies, waits for them, and re-layouts: 41.5 us -> 50.7 us
    all_gather x1 -> x0, waiting for transfers between devices: 31 us -> none  [on_device(): lax.all_gather(mixed, 'ch', axis=1, tiled=True)]
    ppermute x0 -> x7, starting transfers between devices: none -> 13.5 us  [the longest x4 12.2 us: cards_connect(): spare = lax.ppermute(spare, axis_name=across, perm=pool)]
    ppermute x0 -> x7, waiting for transfers between devices: none -> 12.7 us  [the longest x4 12.7 us: cards_connect(): spare = lax.ppermute(spare, axis_name=across, perm=pool)]
    dynamic_update_slice x0 -> x7, local copies, waits for them, and re-layouts: none -> 5.77 us  [the longest x4 3.31 us: cards_connect(): lax.dynamic_update_slice_in_dim(block_next, spare, (val - dd) % m_next *...]
  transfers between devices with their start and end apart: 9 -> 15, of which waited for: 8 -> 11; matrix products, arithmetic and copies ran while one was open for 8% -> 9% of each run, Pallas kernels for 0% -> 0%
where the time goes in v1:
time: 541 us; the launch traced here: 532 us
  waiting for transfers between devices  301 us (56%)
  matrix products  94.2 us (17%)
  starting transfers between devices  74.6 us (14%)
  local copies, waits for them, and re-layouts  50.7 us (9%)
  other arithmetic  11.2 us (2%)
    all_to_all x2, waiting for transfers between devices, sequence_conv(): lax.all_to_all(sectioned[0], 'seq', split_axis=1, concat_axis=2, tiled=True)  95 us
    dot_general x16, matrix products, contract(): return jnp.einsum(pattern, first_op, second_op, precision=highest)  89.8 us
    all_to_all x2, waiting for transfers between devices, sequence_conv(): lax.all_to_all(sectioned[1], 'seq', split_axis=1, concat_axis=2, tiled=True)  88.6 us
    all_to_all x1, waiting for transfers between devices, sequence_conv(): lax.all_to_all(planes, 'seq', split_axis=2, concat_axis=1, tiled=True)  36.6 us
    all_to_all x1, waiting for transfers between devices, sequence_conv(): lax.all_to_all(sectioned[0], 'seq', split_axis=2, concat_axis=1, tiled=True)  34.6 us
    all_to_all x1, waiting for transfers between devices, sequence_conv(): lax.all_to_all(sectioned[1], 'seq', split_axis=2, concat_axis=1, tiled=True)  33.1 us
    all_to_all x2, starting transfers between devices, sequence_conv(): lax.all_to_all(sectioned[1], 'seq', split_axis=1, concat_axis=2, tiled=True)  15.8 us
    all_to_all x2, starting transfers between devices, sequence_conv(): lax.all_to_all(sectioned[0], 'seq', split_axis=1, concat_axis=2, tiled=True)  15 us
  transfers between devices with their start and end apart: 15, of which 11 were waited for; matrix products, arithmetic and copies ran while one was open for 9% of the time, Pallas kernels for 0%

profile of v1, /device:TPU:1, one launch (start us, length us, event | category | flops | bytes accessed | tf_op | source)
XLA Modules:
  0.0 532.0 jit_solution(5726462800146568762)
XLA Ops:
  0.7 4.4 collective-permute-start
  5.1 0.9 fusion.197
  6.0 1.6 maximum_convert_fusion
  8.5 1.5 copy-done.9
  10.2 2.4 copy.68
  12.6 12.5 %all-to-all-start = ((f32[2,1,384,512]{3,0,1,2:T(2,128)}), f32[2,1,384,512]{3,0,1,2:T(2,128)S(1)}, u32[]{:S(2)}, u32[]{:S(2)}) async-start(f32[2,1,384,512]{3,0,1,2:T(2,128)} %copy.68), calls=%async_computation | async-start | bytes 3145728 | tf_op jit(solution)/shard_map/all_to_all | solution.py:55
  25.2 36.6 %all-to-all-done = f32[2,1,384,512]{3,0,1,2:T(2,128)S(1)} async-done(((f32[2,1,384,512]{3,0,1,2:T(2,128)}), f32[2,1,384,512]{3,0,1,2:T(2,128)S(1)}, u32[]{:S(2)}, u32[]{:S(2)}) %all-to-all-start) | async-done | bytes 1572896 | tf_op jit(solution)/shard_map/all_to_all | solution.py:55
  61.9 1.2 fusion.194
  63.9 3.3 fusion.3
  67.1 3.3 fusion.2
  70.4 3.6 convolution_subtract_fusion
  74.0 5.9 %fusion = (f32[4,32,12,512]{3,1,2,0:T(8,128)S(1)}, f32[4,32,12,512]{3,1,2,0:T(8,128)}) fusion(f32[4,12,512,32]{2,3,1,0:T(8,128)S(1)} %convolution_subtract_fusion, f32[32,12]{0,1:T(8,128)S(1)} %get-tuple-element.29, f32[32,12]{0,1:T(8,128)S(1)} %get-tuple-element.28, f32[4,12,512,32]{2,3,1,0:T(8,128)S(1)} %fusion.2, ...), kind=kOutput, calls=%fused_computation.4 | convolution fusion | flops 309868544 | bytes 15731712 | tf_op jit(solution)/shard_map/kp,xpbc->xkbc/dot_general | solution.py:23
  80.0 3.7 copy.79
  83.7 7.3 %all-to-all-start.1 = ((f32[4,32,12,512]{3,0,2,1:T(4,128)}), f32[4,32,12,512]{3,0,2,1:T(4,128)S(1)}, u32[]{:S(2)}, u32[]{:S(2)}) async-start(f32[4,32,12,512]{3,0,2,1:T(4,128)} %copy.79), calls=%async_computation.1 | async-start | bytes 6291456 | tf_op jit(solution)/shard_map/all_to_all | solution.py:74
  91.0 5.5 %copy.81 = f32[4,32,12,512]{3,0,2,1:T(4,128)} copy(f32[4,32,12,512]{3,1,2,0:T(8,128)} %get-tuple-element.10) | data formatting | bytes 6291456 | tf_op jit(solution)/shard_map/add | solution.py:38
  96.5 65.8 %all-to-all-done.1 = f32[4,32,12,512]{3,0,2,1:T(4,128)S(1)} async-done(((f32[4,32,12,512]{3,0,2,1:T(4,128)}), f32[4,32,12,512]{3,0,2,1:T(4,128)S(1)}, u32[]{:S(2)}, u32[]{:S(2)}) %all-to-all-start.1) | async-done | bytes 3145760 | tf_op jit(solution)/shard_map/all_to_all | solution.py:74
  162.3 1.7 copy-done.3
  164.0 7.8 %all-to-all-start.2 = ((f32[4,32,12,512]{3,0,2,1:T(4,128)}), f32[4,32,12,512]{3,0,2,1:T(4,128)}, u32[]{:S(2)}, u32[]{:S(2)}) async-start(f32[4,32,12,512]{3,0,2,1:T(4,128)} %copy.81), calls=%async_computation.2 | async-start | bytes 6291456 | tf_op jit(solution)/shard_map/all_to_all | solution.py:75
  171.9 3.2 copy.80
  175.1 9.8 %fusion.43 = f32[4,512,384]{2,1,0:T(8,128)} fusion(f32[4,384,512]{1,2,0:T(8,128)S(1)} %copy.80), kind=kOutput, calls=%fused_computation.73 | convolution fusion | flops 3625205760 | bytes 6291456 | tf_op jit(solution)/shard_map/mb,xkbc->xkmc/dot_general | solution.py:23
  184.9 60.3 %all-to-all-done.2 = f32[4,32,12,512]{3,0,2,1:T(4,128)} async-done(((f32[4,32,12,512]{3,0,2,1:T(4,128)}), f32[4,32,12,512]{3,0,2,1:T(4,128)}, u32[]{:S(2)}, u32[]{:S(2)}) %all-to-all-start.2) | async-done | bytes 3145760 | tf_op jit(solution)/shard_map/all_to_all | solution.py:75
  245.2 5.2 copy.82
  250.4 10.7 %fusion.41 = f32[4,512,384]{2,1,0:T(8,128)S(1)} fusion(f32[4,384,512]{1,2,0:T(8,128)} %copy.82), kind=kOutput, calls=%fused_computation.71 | convolution fusion | flops 3625205760 | bytes 6291456 | tf_op jit(solution)/shard_map/mb,xkbc->xkmc/dot_general | solution.py:23
  261.1 9.2 %subtract_bitcast_fusion = f32[4,1,384,512]{2,3,0,1:T(8,128)S(1)} fusion(f32[4,512,384]{2,1,0:T(8,128)S(1)} %copy-done.4, f32[4,384,512]{1,2,0:T(8,128)S(1)} %copy-done), kind=kOutput, calls=%fused_computation.9 | convolution fusion | flops 3625992192 | bytes 9437184 | tf_op jit(solution)/shard_map/mb,xkbc->xkmc/dot_general | solution.py:23
  270.4 9.0 %add_bitcast_fusion = f32[4,1,384,512]{2,3,0,1:T(8,128)S(1)} fusion(f32[4,512,384]{2,1,0:T(8,128)S(1)} %fusion.41, f32[4,384,512]{1,2,0:T(8,128)S(1)} %copy.80), kind=kOutput, calls=%fused_computation.8 | convolution fusion | flops 3625992192 | bytes 9437184 | tf_op jit(solution)/shard_map/mb,xkbc->xkmc/dot_general | solution.py:23
  279.7 5.4 %fusion.12 = f32[2,512,384]{2,1,0:T(8,128)S(1)} fusion(f32[2,1,384,512]{2,3,0,1:T(8,128)S(1)} %get-tuple-element.12), kind=kOutput, calls=%fused_computation.30 | convolution fusion | flops 1813266432 | bytes 3145728 | tf_op jit(solution)/shard_map/mb,xkmc->xkbc/dot_general | solution.py:23
  285.1 5.8 %fusion.10 = f32[2,512,384]{2,1,0:T(8,128)S(1)} fusion(f32[2,1,384,512]{2,3,0,1:T(8,128)S(1)} %get-tuple-element.12), kind=kOutput, calls=%fused_computation.28 | convolution fusion | flops 1813266432 | bytes 3145728 | tf_op jit(solution)/shard_map/mb,xkmc->xkbc/dot_general | solution.py:23
  290.9 5.4 %fusion.18 = f32[2,512,384]{2,1,0:T(8,128)S(1)} fusion(f32[2,512,384]{2,1,0:T(8,128)S(1)} %fusion.12, f32[2,1,384,512]{2,3,0,1:T(8,128)S(1)} %get-tuple-element.11), kind=kOutput, calls=%fused_computation.40 | convolution fusion | flops 1813659648 | bytes 4718592 | tf_op jit(solution)/shard_map/mb,xkmc->xkbc/dot_general | solution.py:23
  296.4 5.5 %fusion.7 = (f32[2,1,384,512]{2,3,0,1:T(8,128)S(1)}, f32[2,1,384,512]{2,3,0,1:T(8,128)S(1)}) fusion(f32[2,512,384]{2,1,0:T(8,128)S(1)} %fusion.18, f32[384]{0:T(512)S(1)} %get-tuple-element.34, f32[384]{0:T(512)S(1)} %get-tuple-element.35, f32[2,512,384]{2,1,0:T(8,128)S(1)} %fusion.10, f32[2,1,384,512]{2,3,0,1:T(8,128)S(1)} %get-tuple-element.11), kind=kOutput, calls=%fused_computation.23 | convolution fusion | flops 1816018944 | bytes 7867392 | tf_op jit(solution)/shard_map/mb,xkmc->xkbc/dot_general | solution.py:23
  301.8 2.1 copy.85
  303.9 5.7 %all-to-all-start.3 = ((f32[2,1,384,512]{3,0,1,2:T(2,128)}), f32[2,1,384,512]{3,0,1,2:T(2,128)S(1)}, u32[]{:S(2)}, u32[]{:S(2)}) async-start(f32[2,1,384,512]{3,0,1,2:T(2,128)} %copy.85), calls=%async_computation.3 | async-start | bytes 3145728 | tf_op jit(solution)/shard_map/all_to_all | solution.py:83
  309.7 2.1 copy.87
  311.8 34.6 %all-to-all-done.3 = f32[2,1,384,512]{3,0,1,2:T(2,128)S(1)} async-done(((f32[2,1,384,512]{3,0,1,2:T(2,128)}), f32[2,1,384,512]{3,0,1,2:T(2,128)S(1)}, u32[]{:S(2)}, u32[]{:S(2)}) %all-to-all-start.3) | async-done | bytes 1572896 | tf_op jit(solution)/shard_map/all_to_all | solution.py:83
  346.4 7.7 %all-to-all-start.4 = ((f32[2,1,384,512]{3,0,1,2:T(2,128)}), f32[2,1,384,512]{3,0,1,2:T(2,128)S(1)}, u32[]{:S(2)}, u32[]{:S(2)}) async-start(f32[2,1,384,512]{3,0,1,2:T(2,128)} %copy.87), calls=%async_computation.4 | async-start | bytes 3145728 | tf_op jit(solution)/shard_map/all_to_all | solution.py:84
  354.1 3.7 fusion.28
  357.8 33.1 %all-to-all-done.4 = f32[2,1,384,512]{3,0,1,2:T(2,128)S(1)} async-done(((f32[2,1,384,512]{3,0,1,2:T(2,128)}), f32[2,1,384,512]{3,0,1,2:T(2,128)S(1)}, u32[]{:S(2)}, u32[]{:S(2)}) %all-to-all-start.4) | async-done | bytes 1572896 | tf_op jit(solution)/shard_map/all_to_all | solution.py:84
  390.9 4.0 subtract_bitcast_fusion.1
  394.9 2.4 copy.89
  397.3 7.8 %all-to-all-start.5 = ((f32[2,32,12,512]{3,0,2,1:T(2,128)}), f32[2,32,12,512]{3,0,2,1:T(2,128)}, u32[]{:S(2)}, u32[]{:S(2)}) async-start(f32[2,32,12,512]{3,0,2,1:T(2,128)} %copy.89), calls=%async_computation.5 | async-start | bytes 3145728 | tf_op jit(solution)/shard_map/all_to_all | solution.py:90
  405.1 2.5 fusion.24
  407.6 2.6 add_bitcast_fusion.1
  410.3 2.4 copy.92
  412.7 29.2 %all-to-all-done.5 = f32[2,32,12,512]{3,0,2,1:T(2,128)} async-done(((f32[2,32,12,512]{3,0,2,1:T(2,128)}), f32[2,32,12,512]{3,0,2,1:T(2,128)}, u32[]{:S(2)}, u32[]{:S(2)}) %all-to-all-start.5) | async-done | bytes 1572896 | tf_op jit(solution)/shard_map/all_to_all | solution.py:90
  441.9 8.0 %all-to-all-start.6 = ((f32[2,32,12,512]{3,0,2,1:T(2,128)}), f32[2,32,12,512]{3,0,2,1:T(2,128)}, u32[]{:S(2)}, u32[]{:S(2)}) async-start(f32[2,32,12,512]{3,0,2,1:T(2,128)} %copy.92), calls=%async_computation.6 | async-start | bytes 3145728 | tf_op jit(solution)/shard_map/all_to_all | solution.py:91
  449.9 2.3 broadcast_multiply_fusion
  452.2 4.1 slice_reduce_fusion
  456.4 1.0 squeeze.10
  457.3 1.0 squeeze.9
  458.3 28.3 %all-to-all-done.6 = f32[2,32,12,512]{3,0,2,1:T(2,128)} async-done(((f32[2,32,12,512]{3,0,2,1:T(2,128)}), f32[2,32,12,512]{3,0,2,1:T(2,128)}, u32[]{:S(2)}, u32[]{:S(2)}) %all-to-all-start.6) | async-done | bytes 1572896 | tf_op jit(solution)/shard_map/all_to_all | solution.py:91
  486.7 4.0 fusion.30
  490.7 1.0 squeeze.11
  493.8 1.6 copy-done.8
  495.4 4.8 collective-permute-start.1
  500.2 4.7 collective-permute-done.1
  504.9 2.5 collective-permute-start.3
  507.4 4.7 collective-permute-done.3
  512.1 2.5 collective-permute-start.5
  515.4 1.3 collective-permute-start.6
  517.5 1.8 collective-permute-done.5
  519.3 2.5 collective-permute-start.7
  523.4 0.8 constant_dynamic-update-slice_fusion.2
  525.1 1.4 collective-permute-done.7
  526.5 0.9 constant_dynamic-update-slice_fusion
  527.4 4.4 convolution_convert_fusion
  (49 shorter events, 9.3 us)
Async XLA Ops:
  0.7 5.3 collective-permute-start
  8.3 1.8 copy-start.1
  8.3 1.7 copy-start.9
  12.6 49.3 %all-to-all-start = ((f32[2,1,384,512]{3,0,1,2:T(2,128)}), f32[2,1,384,512]{3,0,1,2:T(2,128)S(1)}, u32[]{:S(2)}, u32[]{:S(2)}) async-start(f32[2,1,384,512]{3,0,1,2:T(2,128)} %copy.68), calls=%async_computation | async-start | bytes 3145728 | tf_op jit(solution)/shard_map/all_to_all | solution.py:55
  83.7 78.6 %all-to-all-start.1 = ((f32[4,32,12,512]{3,0,2,1:T(4,128)}), f32[4,32,12,512]{3,0,2,1:T(4,128)S(1)}, u32[]{:S(2)}, u32[]{:S(2)}) async-start(f32[4,32,12,512]{3,0,2,1:T(4,128)} %copy.79), calls=%async_computation.1 | async-start | bytes 6291456 | tf_op jit(solution)/shard_map/all_to_all | solution.py:74
  162.3 1.7 copy-start.3
  164.0 81.2 %all-to-all-start.2 = ((f32[4,32,12,512]{3,0,2,1:T(4,128)}), f32[4,32,12,512]{3,0,2,1:T(4,128)}, u32[]{:S(2)}, u32[]{:S(2)}) async-start(f32[4,32,12,512]{3,0,2,1:T(4,128)} %copy.81), calls=%async_computation.2 | async-start | bytes 6291456 | tf_op jit(solution)/shard_map/all_to_all | solution.py:75
  250.4 10.7 %copy-start = (f32[4,384,512]{1,2,0:T(8,128)S(1)}, f32[4,384,512]{1,2,0:T(8,128)}, u32[]{:S(2)}) copy-start(f32[4,384,512]{1,2,0:T(8,128)} %copy.82) | copy-start | bytes 9437188
  250.4 10.7 %copy-start.4 = (f32[4,512,384]{2,1,0:T(8,128)S(1)}, f32[4,512,384]{2,1,0:T(8,128)}, u32[]{:S(2)}) copy-start(f32[4,512,384]{2,1,0:T(8,128)} %fusion.43) | copy-start | bytes 9437188
  303.9 42.4 %all-to-all-start.3 = ((f32[2,1,384,512]{3,0,1,2:T(2,128)}), f32[2,1,384,512]{3,0,1,2:T(2,128)S(1)}, u32[]{:S(2)}, u32[]{:S(2)}) async-start(f32[2,1,384,512]{3,0,1,2:T(2,128)} %copy.85), calls=%async_computation.3 | async-start | bytes 3145728 | tf_op jit(solution)/shard_map/all_to_all | solution.py:83
  346.4 44.5 %all-to-all-start.4 = ((f32[2,1,384,512]{3,0,1,2:T(2,128)}), f32[2,1,384,512]{3,0,1,2:T(2,128)S(1)}, u32[]{:S(2)}, u32[]{:S(2)}) async-start(f32[2,1,384,512]{3,0,1,2:T(2,128)} %copy.87), calls=%async_computation.4 | async-start | bytes 3145728 | tf_op jit(solution)/shard_map/all_to_all | solution.py:84
  397.3 44.6 %all-to-all-start.5 = ((f32[2,32,12,512]{3,0,2,1:T(2,128)}), f32[2,32,12,512]{3,0,2,1:T(2,128)}, u32[]{:S(2)}, u32[]{:S(2)}) async-start(f32[2,32,12,512]{3,0,2,1:T(2,128)} %copy.89), calls=%async_computation.5 | async-start | bytes 3145728 | tf_op jit(solution)/shard_map/all_to_all | solution.py:90
  441.9 44.8 %all-to-all-start.6 = ((f32[2,32,12,512]{3,0,2,1:T(2,128)}), f32[2,32,12,512]{3,0,2,1:T(2,128)}, u32[]{:S(2)}, u32[]{:S(2)}) async-start(f32[2,32,12,512]{3,0,2,1:T(2,128)} %copy.92), calls=%async_computation.6 | async-start | bytes 3145728 | tf_op jit(solution)/shard_map/all_to_all | solution.py:91
  490.6 1.9 copy-start.2
  490.7 1.9 copy-start.10
  491.6 1.3 copy-start.5
  491.6 1.5 copy-start.6
  491.6 1.8 copy-start.7
  493.8 1.6 copy-start.8
  495.4 9.5 %collective-permute-start.1 = (bf16[384,512]{1,0:T(8,128)(2,1)S(1)}, bf16[384,512]{1,0:T(8,128)(2,1)S(1)}, u32[]{:S(2)}, u32[]{:S(2)}) collective-permute-start(bf16[384,512]{1,0:T(8,128)(2,1)S(1)} %get-tuple-element.8), channel_id=1, source_target_pairs={{0,1},{1,2},{2,3},{3,4},{4,5},{5,6},{6,7},{7,0},{8,9},{9,10},{10,1... | collective-permute-start | bytes 1179656 | tf_op jit(solution)/shard_map/ppermute | solution.py:110
  500.2 7.2 %collective-permute-start.2 = (bf16[384,512]{1,0:T(8,128)(2,1)S(1)}, bf16[384,512]{1,0:T(8,128)(2,1)S(1)}, u32[]{:S(2)}, u32[]{:S(2)}) collective-permute-start(bf16[384,512]{1,0:T(8,128)(2,1)S(1)} %get-tuple-element.8), channel_id=1, source_target_pairs={{0,7},{1,0},{2,1},{3,2},{4,3},{5,4},{6,5},{7,6},{8,15},{9,8},{10,9... | collective-permute-start | bytes 1179656 | tf_op jit(solution)/shard_map/ppermute | solution.py:115
  504.9 7.2 %collective-permute-start.3 = (bf16[384,512]{1,0:T(8,128)(2,1)S(1)}, bf16[384,512]{1,0:T(8,128)(2,1)S(1)}, u32[]{:S(2)}, u32[]{:S(2)}) collective-permute-start(bf16[384,512]{1,0:T(8,128)(2,1)S(1)} %collective-permute-done.1), channel_id=1, source_target_pairs={{0,1},{1,2},{2,3},{3,4},{4,5},{5,6},{6,7},{7,0},{8,9},{9,10},{10,1... | collective-permute-start | bytes 1179656 | tf_op jit(solution)/shard_map/ppermute | solution.py:110
  507.4 8.0 %collective-permute-start.4 = (bf16[384,512]{1,0:T(8,128)(2,1)S(1)}, bf16[384,512]{1,0:T(8,128)(2,1)S(1)}, u32[]{:S(2)}, u32[]{:S(2)}) collective-permute-start(bf16[384,512]{1,0:T(8,128)(2,1)S(1)} %collective-permute-done.2), channel_id=1, source_target_pairs={{0,7},{1,0},{2,1},{3,2},{4,3},{5,4},{6,5},{7,6},{8,15},{9,8},{10,9... | collective-permute-start | bytes 1179656 | tf_op jit(solution)/shard_map/ppermute | solution.py:115
  512.1 7.2 %collective-permute-start.5 = (bf16[384,512]{1,0:T(8,128)(2,1)S(1)}, bf16[384,512]{1,0:T(8,128)(2,1)S(1)}, u32[]{:S(2)}, u32[]{:S(2)}) collective-permute-start(bf16[384,512]{1,0:T(8,128)(2,1)S(1)} %collective-permute-done.3), channel_id=1, source_target_pairs={{0,1},{1,2},{2,3},{3,4},{4,5},{5,6},{6,7},{7,0},{8,9},{9,10},{10,1... | collective-permute-start | bytes 1179656 | tf_op jit(solution)/shard_map/ppermute | solution.py:110
  515.4 12.0 %copy-start.11 = (bf16[4096,512]{1,0:T(8,128)(2,1)S(1)}, bf16[4096,512]{1,0:T(8,128)(2,1)}, u32[]{:S(2)}) copy-start(bf16[4096,512]{1,0:T(8,128)(2,1)} %param.13) | copy-start | bytes 12582916
  515.4 8.9 %collective-permute-start.6 = (bf16[384,512]{1,0:T(8,128)(2,1)S(1)}, bf16[384,512]{1,0:T(8,128)(2,1)S(1)}, u32[]{:S(2)}, u32[]{:S(2)}) collective-permute-start(bf16[384,512]{1,0:T(8,128)(2,1)S(1)} %collective-permute-done.4), channel_id=1, source_target_pairs={{0,7},{1,0},{2,1},{3,2},{4,3},{5,4},{6,5},{7,6},{8,15},{9,8},{10,9... | collective-permute-start | bytes 1179656 | tf_op jit(solution)/shard_map/ppermute | solution.py:115
  519.3 7.2 %collective-permute-start.7 = (bf16[384,512]{1,0:T(8,128)(2,1)S(1)}, bf16[384,512]{1,0:T(8,128)(2,1)S(1)}, u32[]{:S(2)}, u32[]{:S(2)}) collective-permute-start(bf16[384,512]{1,0:T(8,128)(2,1)S(1)} %collective-permute-done.5), channel_id=1, source_target_pairs={{0,1},{1,2},{2,3},{3,4},{4,5},{5,6},{6,7},{7,0},{8,9},{9,10},{10,1... | collective-permute-start | bytes 1179656 | tf_op jit(solution)/shard_map/ppermute | solution.py:110
